TPU v7x, 32 devices: a whole 2x2x4 slice. The times are simulated.
32 devices in a mesh: groups: 2 (over y), deg: 4 (over z), sub: 2 (over x), fld: 2 (over core).
Axes of the slice: x: 2, y: 2, z: 4, core: 2. Of those that a mesh axis runs over, the one named last changes fastest.
Arguments:
- coefficients: bfloat16 [32, 2, 32, 2048], P(None, None, ('groups', 'fld'), ('deg', 'sub')), parts along dimension 2, may hold values from -6 to 6
- delta: bfloat16 [32, 2, 2048, 2048], P('deg', None, None, 'sub'), may hold values from -0.125 to 0.125
- order_of: int32 [2048], replicated, may hold values from 0 to 2047, each once
- degree_of: int32 [32], replicated, may hold values from 512 to 2047
- angle_index: int32 [32, 3], P(('groups', 'fld')), parts along dimension 0, may hold values from 0 to 4095
Outputs:
- rotated: float32 [32, 2, 32, 2048], P(None, None, ('groups', 'fld'), ('deg', 'sub')), parts along dimension 2
There are 2 independent parts, one for each index of `groups`. A program takes and returns all parts, laid end to end along the dimension named above; an argument that names none is the same for every part. Nothing has to cross between parts.
All inputs are finite; a program needn't handle non-finite values.
Results may differ from a plain program's by a relative error of at most 0.004.
Values may be sent and summed in bfloat16 or wider, within the bound.
No kernel may reach another device: no remote copies, remote signals or barrier semaphores. Data moves between devices by JAX's collectives and lax.ppermute only.
A program may use at most 128 MiB of HBM per device.

v0:
```python
import math
import jax
import jax.numpy as jnp
from jax import lax
from jax.sharding import PartitionSpec as P

NM = 2048
NANG = 4096


def phase_pair(angle_index, column, orders):
    steps_int = angle_index[:, column][:, None] * orders[None, :] % NANG
    angle_val = steps_int.astype(jnp.float32) * (2.0 * math.pi / NANG)
    return (jnp.cos(angle_val), jnp.sin(angle_val))


def twist_phase(values, cosine, sine):
    cos_part = values[:, 0]
    sin_part = values[:, 1]
    return jnp.stack(
        [cosine * cos_part - sine * sin_part, sine * cos_part + cosine * sin_part], axis=1
    )


def live_mask(degrees, orders):
    limits = degrees[:, None]
    cosine_live = orders[None, :] <= limits
    sine_live = cosine_live & (orders[None, :] >= 1)
    return jnp.stack([cosine_live, sine_live], axis=1)[:, :, None, :].astype(jnp.float32)


def per_device(coefficients, delta, order_of, degree_of, angle_index):
    deg_size = lax.axis_size("deg")
    sub_size = lax.axis_size("sub")
    deg_count = delta.shape[0]
    col_count = delta.shape[3]
    slot_count = coefficients.shape[3]
    slot_ids = jnp.arange(NM, dtype=jnp.int32)
    inverse = jnp.zeros((NM,), jnp.int32).at[order_of].set(slot_ids)
    widened = lax.all_gather(coefficients, "sub", axis=3, tiled=True)
    slot_rows = lax.all_to_all(widened, "deg", split_axis=0, concat_axis=3, tiled=True)
    natural = jnp.take(slot_rows, inverse, axis=3)
    my_degrees = lax.dynamic_slice_in_dim(degree_of, lax.axis_index("deg") * deg_count, deg_count)
    gamma_cos, gamma_sin = phase_pair(angle_index, 2, slot_ids)
    first_turn = twist_phase(
        live_mask(my_degrees, slot_ids) * natural.astype(jnp.float32), gamma_cos, gamma_sin
    ).astype(jnp.bfloat16)
    product = jnp.einsum("kpfm,kpmn->kpfn", first_turn, delta, preferred_element_type=jnp.float32)
    col_orders = lax.axis_index("sub") * col_count + jnp.arange(col_count, dtype=jnp.int32)
    col_live = live_mask(my_degrees, col_orders)
    beta_cos, beta_sin = phase_pair(angle_index, 1, col_orders)
    middle = twist_phase(col_live * product, beta_cos, beta_sin).astype(jnp.bfloat16)
    second = jnp.einsum(
        "kpfm,kpmn->kpfn",
        lax.all_gather(middle, "sub", axis=3, tiled=True),
        delta,
        preferred_element_type=jnp.float32,
    )
    alpha_cos, alpha_sin = phase_pair(angle_index, 0, col_orders)
    result = twist_phase(col_live * second, alpha_cos, alpha_sin)
    full_cols = lax.all_gather(result, "sub", axis=3, tiled=True)
    slot_table = order_of.reshape(deg_size, sub_size, slot_count)
    pick_slots = lax.dynamic_index_in_dim(
        slot_table, lax.axis_index("sub"), 1, keepdims=False
    ).reshape(-1)
    picked = jnp.take(full_cols, pick_slots, axis=3)
    gathered = lax.all_to_all(picked, "deg", split_axis=3, concat_axis=0, tiled=True)
    return gathered


def solution(mesh):
    in_specs = (
        P(None, None, ("groups", "fld"), ("deg", "sub")),
        P("deg", None, None, "sub"),
        P(),
        P(),
        P(("groups", "fld"), None),
    )
    out_specs = P(None, None, ("groups", "fld"), ("deg", "sub"))
    return jax.shard_map(
        per_device, mesh=mesh, in_specs=in_specs, out_specs=out_specs, check_vma=False
    )
```

profile of v0, /device:TPU:0, one launch (start us, length us, event | category | flops | bytes accessed | tf_op | source)
XLA Modules:
  0.0 229.7 jit_solution(14669175599531877620)
XLA Ops:
  6.5 11.9 %all_gather.9 = bf16[32,2,8,512]{3,2,1,0:T(8,128)(2,1)} all-gather(bf16[32,2,8,256]{3,2,1,0:T(8,128)(2,1)} %param.5), channel_id=1, replica_groups=mesh['groups'=2,'deg'=4,'sub'=2,'fld'=2] {'sub'}, dimensions={3}, use_global_device_ids=true | all-gather | bytes 786432 | tf_op jit(solution)/shard_map/all_gather | solution.py:40
  18.4 4.9 %all-to-all-start = ((bf16[32,2,8,512]{3,2,1,0:T(8,128)(2,1)}), bf16[32,2,8,512]{3,2,1,0:T(8,128)(2,1)S(1)}, u32[]{:S(2)}, u32[]{:S(2)}) async-start(bf16[32,2,8,512]{3,2,1,0:T(8,128)(2,1)} %all_gather.9), calls=%async_computation | async-start | bytes 1048576 | tf_op jit(solution)/shard_map/all_to_all | solution.py:41
  23.3 0.0 all-gather.2.cloned.1.call-start
  23.3 0.7 compare_select_fusion.2
  24.0 8.0 %scatter_custom_fusion = s32[2048]{0:T(1024)S(1)} fusion(s32[2048]{0:T(1024)S(1)} %compare_select_fusion.2, s32[2048]{0:T(1024)S(1)} %iota.33, s32[]{:T(128)} %constant.69.clone.1), kind=kCustom, calls=%fused_computation.63 | custom fusion | bytes 8196 | tf_op jit(solution)/shard_map/scatter | solution.py:39
  32.1 0.8 slice_bitcast_fusion.2
  32.9 0.7 dynamic_slice.8
  33.7 0.2 iota_compare_fusion
  33.8 0.1 broadcast_compare_fusion
  33.9 0.2 add_convert_fusion.2
  34.1 0.1 copy.12
  34.2 0.3 fusion.20
  34.5 0.3 fusion.16
  34.9 2.3 %all-to-all-done = bf16[32,2,8,512]{3,2,1,0:T(8,128)(2,1)S(1)} async-done(((bf16[32,2,8,512]{3,2,1,0:T(8,128)(2,1)}), bf16[32,2,8,512]{3,2,1,0:T(8,128)(2,1)S(1)}, u32[]{:S(2)}, u32[]{:S(2)}) %all-to-all-start) | async-done | bytes 524320 | tf_op jit(solution)/shard_map/all_to_all | solution.py:41
  37.2 0.4 copy.20
  37.6 6.4 %copy.18 = bf16[8,2,8,4,512]{2,0,4,3,1:T(8,128)(2,1)} copy(bf16[8,2,8,4,512]{4,3,2,1,0:T(4,128)(2,1)S(1)} %bitcast.33) | data formatting | bytes 1048576 | tf_op jit(solution)/shard_map/all_to_all | solution.py:41
  44.0 19.9 %gather_fusion = bf16[2048,8,2,8]{3,1,2,0:T(8,128)(2,1)} fusion(bf16[8,2,8,2048]{2,0,3,1:T(8,128)(2,1)} %bitcast.32, s32[2048]{0:T(1024)S(1)} %fusion.21), kind=kCustom, calls=%fused_computation | custom fusion | bytes 1056768 | tf_op jit(solution)/shard_map/jit(_take)/gather | solution.py:42
  63.9 8.3 %copy.15 = bf16[2048,8,2,8]{0,3,2,1:T(8,128)(2,1)S(1)} copy(bf16[2048,8,2,8]{3,1,2,0:T(8,128)(2,1)} %gather_fusion) | data formatting | bytes 1048576 | tf_op jit(solution)/shard_map/jit(_take)/gather | solution.py:42
  72.2 0.1 bitcast_multiply_fusion
  72.3 0.1 subtract_convert_fusion
  72.5 22.6 %convolution_multiply_fusion.1 = f32[8,2,8,1024]{3,2,1,0:T(8,128)S(1)} fusion(bf16[8,2,2048,1024]{3,2,1,0:T(8,128)(2,1)} %param.6, bf16[8,1,8,2048]{3,2,1,0:T(8,128)(2,1)S(1)} %get-tuple-element.6, bf16[8,1,8,2048]{3,2,1,0:T(8,128)(2,1)S(1)} %get-tuple-element.5, f32[8,2,1024]{2,1,0:T(2,128)S(1)} %copy.12), kind=kOutput, calls=%fused_computation.5 | convolution fusion | flops 537264128 | bytes 68222976 | tf_op jit(solution)/shard_map/kpfm,kpmn->kpfn/dot_general | solution.py:48
  95.1 0.1 subtract_convert_fusion.1
  95.2 8.2 %all_gather.10 = bf16[8,2,8,2048]{3,2,1,0:T(8,128)(2,1)S(1)} all-gather(bf16[8,2,8,1024]{3,2,1,0:T(8,128)(2,1)S(1)} %pad_maximum_fusion.1), channel_id=1, replica_groups=mesh['groups'=2,'deg'=4,'sub'=2,'fld'=2] {'sub'}, dimensions={3}, use_global_device_ids=true | all-gather | bytes 786432 | tf_op jit(solution)/shard_map/all_gather | solution.py:55
  103.4 0.0 copy-start
  103.4 22.6 %convolution_multiply_fusion = f32[8,2,8,1024]{3,2,1,0:T(8,128)S(1)} fusion(bf16[8,2,8,2048]{3,2,1,0:T(8,128)(2,1)S(1)} %all_gather.10, bf16[8,2,2048,1024]{3,2,1,0:T(8,128)(2,1)} %param.6, f32[8,2,1024]{2,1,0:T(2,128)S(1)} %copy.12), kind=kOutput, calls=%fused_computation.4 | convolution fusion | flops 537001984 | bytes 68222976 | tf_op jit(solution)/shard_map/kpfm,kpmn->kpfn/dot_general | solution.py:53
  126.0 0.1 multiply_subtract_fusion
  126.1 0.8 pad_maximum_fusion
  126.9 0.0 all-gather.2.cloned.1.call-update
  127.0 0.0 copy-done
  127.0 19.1 %all-gather.2.cloned.1.call-done = f32[8,2,8,2048]{3,2,1,0:T(8,128)} async-done(((f32[8,2,8,1024]{3,2,1,0:T(8,128)}), f32[8,2,8,2048]{3,2,1,0:T(8,128)}) %all-gather.2.cloned.1.call-update) | async-done | bytes 1048592 | tf_op jit(solution)/shard_map/all_gather | solution.py:61
  146.2 9.7 %copy.16 = f32[8,2,8,2048]{2,0,3,1:T(8,128)} copy(f32[8,2,8,2048]{3,2,1,0:T(8,128)} %all-gather.2.cloned.1.call-done) | data formatting | bytes 2097152 | tf_op jit(solution)/shard_map/all_gather | solution.py:61
  155.9 15.4 %gather_fusion.1 = f32[1024,8,2,8]{3,1,2,0:T(8,128)} fusion(f32[8,2,8,2048]{2,0,3,1:T(8,128)} %copy.16, s32[1024]{0:T(1024)S(1)} %broadcast_clamp_fusion), kind=kCustom, calls=%fused_computation.1 | custom fusion | bytes 1052672 | tf_op jit(solution)/shard_map/jit(_take)/gather | solution.py:66
  171.3 8.7 %fusion.25 = f32[1024,2,8,8]{3,2,1,0:T(8,128)} fusion(f32[1024,8,2,8]{3,1,2,0:T(8,128)} %gather_fusion.1, pred[1024]{0:T(1024)(128)(4,1)S(1)} %compare_and_fusion.1), kind=kLoop, calls=%fused_computation.74 | loop fusion | flops 131072 | bytes 1049600
  180.0 6.6 %reshape.470 = f32[4,1,32768]{2,1,0:T(1,128)S(1)} reshape(f32[1024,2,8,8]{3,2,1,0:T(8,128)} %fusion.25) | data formatting | bytes 1048576
  186.6 18.7 %all_to_all.36 = f32[4,1,32768]{2,1,0:T(1,128)S(1)} all-to-all(f32[4,1,32768]{2,1,0:T(1,128)S(1)} %reshape.470), channel_id=1, replica_groups=mesh['groups'=2,'deg'=4,'sub'=2,'fld'=2] {'deg'}, dimensions={0} | all-to-all | bytes 1048576 | tf_op jit(solution)/shard_map/all_to_all | solution.py:67
  205.3 0.5 broadcast.453
  205.9 2.1 reduce
  208.0 7.9 %reshape.471 = f32[1024,2,8,8]{3,2,1,0:T(8,128)} reshape(f32[4,32768]{1,0:T(4,128)S(1)} %reduce) | data formatting | bytes 1048576
  215.9 6.9 %copy.17 = f32[4,8,2,8,256]{4,3,2,1,0:T(8,128)} copy(f32[4,8,2,8,256]{3,1,2,4,0:T(8,128)} %bitcast.31) | data formatting | bytes 1048576 | tf_op jit(solution)/shard_map/all_to_all | solution.py:67
  (13 shorter events, 0.1 us)
Async XLA Ops:
  18.4 18.8 %all-to-all-start = ((bf16[32,2,8,512]{3,2,1,0:T(8,128)(2,1)}), bf16[32,2,8,512]{3,2,1,0:T(8,128)(2,1)S(1)}, u32[]{:S(2)}, u32[]{:S(2)}) async-start(bf16[32,2,8,512]{3,2,1,0:T(8,128)(2,1)} %all_gather.9), calls=%async_computation | async-start | bytes 1048576 | tf_op jit(solution)/shard_map/all_to_all | solution.py:41
  23.3 122.9 %all-gather.2.cloned.1.call-start = ((), (), s32[]{:S(2)}) async-start(), calls=%async_computation.2 | async-start | bytes 1572864 | tf_op jit(solution)/shard_map/all_gather | solution.py:61
  103.4 23.6 %copy-start = (s32[2048]{0:T(1024)S(1)}, s32[2048]{0:T(1024)}, u32[]{:S(2)}) copy-start(s32[2048]{0:T(1024)} %param.7) | copy-start | bytes 24580
Sparse Core Ops, SparseCore 0:
  127.1 19.0 all-gather.1
where the time goes:
time: 231 us; the launch traced here: 230 us
  local copies, waits for them, and re-layouts  91.7 us (40%)
  matrix products  45.3 us (20%)
  blocking collectives  38.8 us (17%)
  waiting for transfers between devices  21.5 us (9%)
  other arithmetic  14 us (6%)
  between operations  13.6 us (6%)
  starting transfers between devices  4.87 us (2%)
    gather x2, local copies, waits for them, and re-layouts, per_device(): natural = jnp.take(slot_rows, inverse, axis=3)  28.2 us
    dot_general x1, matrix products, per_device(): jnp.einsum('kpfm,kpmn->kpfn', lax.all_gather(middle, 'sub', axis=3, tiled...  22.6 us
    dot_general x1, matrix products, per_device(): jnp.einsum('kpfm,kpmn->kpfn', first_turn, delta, preferred_element_type=j...  22.6 us
    all_gather x1, waiting for transfers between devices, per_device(): full_cols = lax.all_gather(result, 'sub', axis=3, tiled=True)  19.1 us
    all_to_all x1, blocking collectives, per_device(): lax.all_to_all(picked, 'deg', split_axis=3, concat_axis=0, tiled=True)  18.7 us
    gather x1, local copies, waits for them, and re-layouts, per_device(): picked = jnp.take(full_cols, pick_slots, axis=3)  15.4 us
    unnamed x4, local copies, waits for them, and re-layouts  14.5 us
    all_gather x1, blocking collectives, per_device(): widened = lax.all_gather(coefficients, 'sub', axis=3, tiled=True)  11.9 us
  transfers between devices with their start and end apart: 2, of which 2 were waited for; matrix products, arithmetic and copies ran while one was open for 5% of the time, Pallas kernels for 0%

commit v1 on v0

--- a/solution.py
+++ b/solution.py
@@ -58,7 +58,7 @@
     )
     alpha_cos, alpha_sin = phase_pair(angle_index, 0, col_orders)
     result = twist_phase(col_live * second, alpha_cos, alpha_sin)
-    full_cols = lax.all_gather(result, "sub", axis=3, tiled=True)
+    full_cols = jnp.concatenate(lax.all_gather(result, "sub"), axis=3)
     slot_table = order_of.reshape(deg_size, sub_size, slot_count)
     pick_slots = lax.dynamic_index_in_dim(
         slot_table, lax.axis_index("sub"), 1, keepdims=False

time: 231 us -> 230 us (level)
    reshape x0 -> x1, local copies, waits for them, and re-layouts: none -> 8.47 us  [per_device(): full_cols = jnp.concatenate(lax.all_gather(result, 'sub'), axis=3)]
    all_gather x1, local copies, waits for them, and re-layouts: 9.75 us -> 2.04 us  [per_device(): full_cols = jnp.concatenate(lax.all_gather(result, 'sub'), axis=3)]
    all_to_all x2 -> x3, local copies, waits for them, and re-layouts: 7.43 us -> 6.64 us  [per_device(): lax.all_to_all(picked, 'deg', split_axis=3, concat_axis=0, tiled=True)]
where the time goes in v1:
time: 230 us
  local copies, waits for them, and re-layouts  91.7 us (40%)
  matrix products  45.3 us (20%)
  blocking collectives  38.8 us (17%)
  waiting for transfers between devices  21.5 us (9%)
  other arithmetic  14 us (6%)
  between operations  13.6 us (6%)
  starting transfers between devices  4.87 us (2%)
    gather x2, local copies, waits for them, and re-layouts, per_device(): natural = jnp.take(slot_rows, inverse, axis=3)  28.2 us
    dot_general x1, matrix products, per_device(): jnp.einsum('kpfm,kpmn->kpfn', lax.all_gather(middle, 'sub', axis=3, tiled...  22.6 us
    dot_general x1, matrix products, per_device(): jnp.einsum('kpfm,kpmn->kpfn', first_turn, delta, preferred_element_type=j...  22.6 us
    all_gather x1, waiting for transfers between devices, per_device(): full_cols = jnp.concatenate(lax.all_gather(result, 'sub'), axis=3)  19.1 us
    all_to_all x1, blocking collectives, per_device(): lax.all_to_all(picked, 'deg', split_axis=3, concat_axis=0, tiled=True)  18.7 us
    gather x1, local copies, waits for them, and re-layouts, per_device(): picked = jnp.take(full_cols, pick_slots, axis=3)  15.4 us
    unnamed x4, local copies, waits for them, and re-layouts  14.5 us
    all_gather x1, blocking collectives, per_device(): widened = lax.all_gather(coefficients, 'sub', axis=3, tiled=True)  11.9 us
  transfers between devices with their start and end apart: 2, of which 2 were waited for; matrix products, arithmetic and copies ran while one was open for 5% of the time, Pallas kernels for 0%

profile of v1, /device:TPU:0, one launch (start us, length us, event | category | flops | bytes accessed | tf_op | source)
XLA Modules:
  0.0 229.7 jit_solution(11736378691079202638)
XLA Ops:
  6.5 11.9 %all_gather.12 = bf16[32,2,8,512]{3,2,1,0:T(8,128)(2,1)} all-gather(bf16[32,2,8,256]{3,2,1,0:T(8,128)(2,1)} %param.5), channel_id=1, replica_groups=mesh['groups'=2,'deg'=4,'sub'=2,'fld'=2] {'sub'}, dimensions={3}, use_global_device_ids=true | all-gather | bytes 786432 | tf_op jit(solution)/shard_map/all_gather | solution.py:40
  18.4 4.9 %all-to-all-start = ((bf16[32,2,8,512]{3,2,1,0:T(8,128)(2,1)}), bf16[32,2,8,512]{3,2,1,0:T(8,128)(2,1)S(1)}, u32[]{:S(2)}, u32[]{:S(2)}) async-start(bf16[32,2,8,512]{3,2,1,0:T(8,128)(2,1)} %all_gather.12), calls=%async_computation | async-start | bytes 1048576 | tf_op jit(solution)/shard_map/all_to_all | solution.py:41
  23.3 0.0 all-gather.3.cloned.1.call-start
  23.3 0.7 compare_select_fusion.2
  24.0 8.0 %scatter_custom_fusion = s32[2048]{0:T(1024)S(1)} fusion(s32[2048]{0:T(1024)S(1)} %compare_select_fusion.2, s32[2048]{0:T(1024)S(1)} %iota.33, s32[]{:T(128)} %constant.69.clone.1), kind=kCustom, calls=%fused_computation.64 | custom fusion | bytes 8196 | tf_op jit(solution)/shard_map/scatter | solution.py:39
  32.1 0.8 slice_bitcast_fusion.2
  32.9 0.7 dynamic_slice.8
  33.7 0.2 iota_compare_fusion
  33.8 0.1 broadcast_compare_fusion
  33.9 0.2 add_convert_fusion.2
  34.1 0.1 copy.26
  34.2 0.3 fusion.20
  34.5 0.3 fusion.16
  34.9 2.3 %all-to-all-done = bf16[32,2,8,512]{3,2,1,0:T(8,128)(2,1)S(1)} async-done(((bf16[32,2,8,512]{3,2,1,0:T(8,128)(2,1)}), bf16[32,2,8,512]{3,2,1,0:T(8,128)(2,1)S(1)}, u32[]{:S(2)}, u32[]{:S(2)}) %all-to-all-start) | async-done | bytes 524320 | tf_op jit(solution)/shard_map/all_to_all | solution.py:41
  37.2 0.4 copy.40
  37.6 6.4 %copy.34 = bf16[8,2,8,4,512]{2,0,4,3,1:T(8,128)(2,1)} copy(bf16[8,2,8,4,512]{4,3,2,1,0:T(4,128)(2,1)S(1)} %bitcast.39) | data formatting | bytes 1048576 | tf_op jit(solution)/shard_map/all_to_all | solution.py:41
  44.0 19.9 %gather_fusion = bf16[2048,8,2,8]{3,1,2,0:T(8,128)(2,1)} fusion(bf16[8,2,8,2048]{2,0,3,1:T(8,128)(2,1)} %bitcast.37, s32[2048]{0:T(1024)S(1)} %fusion.21), kind=kCustom, calls=%fused_computation | custom fusion | bytes 1056768 | tf_op jit(solution)/shard_map/jit(_take)/gather | solution.py:42
  63.9 8.3 %copy.29 = bf16[2048,8,2,8]{0,3,2,1:T(8,128)(2,1)S(1)} copy(bf16[2048,8,2,8]{3,1,2,0:T(8,128)(2,1)} %gather_fusion) | data formatting | bytes 1048576 | tf_op jit(solution)/shard_map/jit(_take)/gather | solution.py:42
  72.2 0.1 bitcast_multiply_fusion
  72.3 0.1 subtract_convert_fusion
  72.5 22.6 %convolution_multiply_fusion.1 = f32[8,2,8,1024]{3,2,1,0:T(8,128)S(1)} fusion(bf16[8,2,2048,1024]{3,2,1,0:T(8,128)(2,1)} %param.6, bf16[8,1,8,2048]{3,2,1,0:T(8,128)(2,1)S(1)} %get-tuple-element.6, bf16[8,1,8,2048]{3,2,1,0:T(8,128)(2,1)S(1)} %get-tuple-element.5, f32[8,2,1024]{2,1,0:T(2,128)S(1)} %copy.26), kind=kOutput, calls=%fused_computation.5 | convolution fusion | flops 537264128 | bytes 68222976 | tf_op jit(solution)/shard_map/kpfm,kpmn->kpfn/dot_general | solution.py:48
  95.1 0.1 subtract_convert_fusion.1
  95.2 8.2 %all_gather.13 = bf16[8,2,8,2048]{3,2,1,0:T(8,128)(2,1)S(1)} all-gather(bf16[8,2,8,1024]{3,2,1,0:T(8,128)(2,1)S(1)} %pad_maximum_fusion.1), channel_id=1, replica_groups=mesh['groups'=2,'deg'=4,'sub'=2,'fld'=2] {'sub'}, dimensions={3}, use_global_device_ids=true | all-gather | bytes 786432 | tf_op jit(solution)/shard_map/all_gather | solution.py:55
  103.4 0.0 copy-start
  103.4 22.6 %convolution_multiply_fusion = f32[8,2,8,1024]{3,2,1,0:T(8,128)S(1)} fusion(bf16[8,2,8,2048]{3,2,1,0:T(8,128)(2,1)S(1)} %all_gather.13, bf16[8,2,2048,1024]{3,2,1,0:T(8,128)(2,1)} %param.6, f32[8,2,1024]{2,1,0:T(2,128)S(1)} %copy.26), kind=kOutput, calls=%fused_computation.4 | convolution fusion | flops 537001984 | bytes 68222976 | tf_op jit(solution)/shard_map/kpfm,kpmn->kpfn/dot_general | solution.py:53
  126.0 0.1 multiply_subtract_fusion
  126.1 0.8 pad_maximum_fusion
  126.9 0.0 all-gather.3.cloned.1.call-update
  127.0 0.0 copy-done
  127.0 19.1 %all-gather.3.cloned.1.call-done = f32[16,2,8,1024]{3,2,1,0:T(8,128)} async-done(((f32[8,2,8,1024]{3,2,1,0:T(8,128)}), f32[16,2,8,1024]{3,2,1,0:T(8,128)}) %all-gather.3.cloned.1.call-update) | async-done | bytes 1048592 | tf_op jit(solution)/shard_map/all_gather | solution.py:61
  146.2 2.0 copy.39
  148.2 8.5 %copy.35 = f32[8,2,8,2,1024]{2,0,4,3,1:T(8,128)} copy(f32[8,2,8,2,1024]{4,3,2,1,0:T(2,128)S(1)} %bitcast.38) | data formatting | bytes 2097152 | tf_op jit(solution)/shard_map/reshape | solution.py:61
  156.7 15.4 %gather_fusion.1 = f32[1024,8,2,8]{3,1,2,0:T(8,128)} fusion(f32[8,2,8,2048]{2,0,3,1:T(8,128)} %bitcast.36, s32[1024]{0:T(1024)S(1)} %broadcast_clamp_fusion), kind=kCustom, calls=%fused_computation.1 | custom fusion | bytes 1052672 | tf_op jit(solution)/shard_map/jit(_take)/gather | solution.py:66
  172.1 8.7 %fusion.25 = f32[1024,2,8,8]{3,2,1,0:T(8,128)} fusion(f32[1024,8,2,8]{3,1,2,0:T(8,128)} %gather_fusion.1, pred[1024]{0:T(1024)(128)(4,1)S(1)} %compare_and_fusion.1), kind=kLoop, calls=%fused_computation.75 | loop fusion | flops 131072 | bytes 1049600
  180.8 6.6 %reshape.479 = f32[4,1,32768]{2,1,0:T(1,128)S(1)} reshape(f32[1024,2,8,8]{3,2,1,0:T(8,128)} %fusion.25) | data formatting | bytes 1048576
  187.4 18.7 %all_to_all.36 = f32[4,1,32768]{2,1,0:T(1,128)S(1)} all-to-all(f32[4,1,32768]{2,1,0:T(1,128)S(1)} %reshape.479), channel_id=1, replica_groups=mesh['groups'=2,'deg'=4,'sub'=2,'fld'=2] {'deg'}, dimensions={0} | all-to-all | bytes 1048576 | tf_op jit(solution)/shard_map/all_to_all | solution.py:67
  206.1 0.5 broadcast.453
  206.6 2.1 reduce
  208.8 7.9 %reshape.480 = f32[1024,2,8,8]{3,2,1,0:T(8,128)} reshape(f32[4,32768]{1,0:T(4,128)S(1)} %reduce) | data formatting | bytes 1048576
  216.7 5.2 %copy.36 = f32[8,2,8,4,256]{4,3,2,1,0:T(4,128)S(1)} copy(f32[8,2,8,4,256]{2,0,1,4,3:T(8,128)} %bitcast.35) | data formatting | bytes 1048576 | tf_op jit(solution)/shard_map/all_to_all | solution.py:67
  221.9 0.9 copy.33
  (13 shorter events, 0.1 us)
Async XLA Ops:
  18.4 18.8 %all-to-all-start = ((bf16[32,2,8,512]{3,2,1,0:T(8,128)(2,1)}), bf16[32,2,8,512]{3,2,1,0:T(8,128)(2,1)S(1)}, u32[]{:S(2)}, u32[]{:S(2)}) async-start(bf16[32,2,8,512]{3,2,1,0:T(8,128)(2,1)} %all_gather.12), calls=%async_computation | async-start | bytes 1048576 | tf_op jit(solution)/shard_map/all_to_all | solution.py:41
  23.3 122.9 %all-gather.3.cloned.1.call-start = ((), (), s32[]{:S(2)}) async-start(), calls=%async_computation.2 | async-start | bytes 1572864 | tf_op jit(solution)/shard_map/all_gather | solution.py:61
  103.4 23.6 %copy-start = (s32[2048]{0:T(1024)S(1)}, s32[2048]{0:T(1024)}, u32[]{:S(2)}) copy-start(s32[2048]{0:T(1024)} %param.7) | copy-start | bytes 24580
Sparse Core Ops, SparseCore 0:
  127.1 19.0 all-gather.2
